TPU v7x, 32 devices: a whole 2x2x4 slice. The times are simulated.
32 devices in a mesh: brow: 4 (over y, x), bcol: 8 (over z, core).
Axes of the slice: x: 2, y: 2, z: 4, core: 2. Of those that a mesh axis runs over, the one named last changes fastest.
Arguments:
- gradient: bfloat16 [2048, 2048], P(('brow', 'bcol')), may hold values from -1.5 to 1.5
- left_stats: float32 [4, 2048, 512], P('brow', 'bcol'), may hold values from -1 to 8, as said below
- right_stats: float32 [4, 2048, 512], P('brow', 'bcol'), may hold values from -1 to 8, as said below
- left_roots: bfloat16 [4, 2048, 512], P('brow', 'bcol'), may hold values from -1 to 3, as said below
- right_roots: bfloat16 [4, 2048, 512], P('brow', 'bcol'), may hold values from -1 to 3, as said below
- refresh: int32 [4, 1], P('brow'), may hold values from 0 to 3, as said below
Outputs:
- update: bfloat16 [2048, 2048], P(('brow', 'bcol'))
- new_left_stats: float32 [4, 2048, 512], P('brow', 'bcol')
- new_right_stats: float32 [4, 2048, 512], P('brow', 'bcol')
- new_left_roots: bfloat16 [4, 2048, 512], P('brow', 'bcol')
- new_right_roots: bfloat16 [4, 2048, 512], P('brow', 'bcol')
Inputs may be any that keep to these rules, and one draw needn't show every extreme that they name: `refresh`: each row names 1 different block columns; some block row lists column 3 and another block row lists column 0. `left_stats`: every 512 x 512 block is symmetric positive definite. `right_stats`: every 512 x 512 block is symmetric positive definite. `left_roots`: every 512 x 512 block is symmetric. `right_roots`: every 512 x 512 block is symmetric.
All inputs are finite; a program needn't handle non-finite values.
Results may differ from a plain program's by a relative error of at most 0.005.
Values may be sent and summed in bfloat16 or wider, within the bound.
No kernel may reach another device: no remote copies, remote signals or barrier semaphores. Data moves between devices by JAX's collectives and lax.ppermute only.
A program may use at most 64 MiB of HBM per device.

v0:
```python
import jax
import jax.numpy as jnp
from jax import lax
from jax.sharding import PartitionSpec as P

ITERS = 3
decay = 0.9
epsilon = 1e-06
highest = lax.Precision.HIGHEST


def from_partner(shard, axis, stride):
    return lax.ppermute(shard, axis, [(i, i ^ 1 << stride) for i in range(lax.axis_size(axis))])


def product(left_side, right_side):
    return jnp.dot(left_side, right_side, precision=highest)


def unchanged(matrix):
    return matrix


def inverse_rows(row_block, collect):
    row_count, order_size = row_block.shape
    eye_rows = (
        lax.broadcasted_iota(jnp.int32, (row_count, order_size), 0)
        == lax.broadcasted_iota(jnp.int32, (row_count, order_size), 1)
    ).astype(jnp.float32)
    eye_full = jnp.eye(order_size, dtype=jnp.float32)
    shifted = row_block + epsilon * eye_rows
    whole_matrix = collect(shifted)
    scaling = 2.5 / jnp.sqrt(jnp.sum(whole_matrix * whole_matrix))
    moment_full = scaling * whole_matrix
    iterate = jnp.sqrt(jnp.sqrt(scaling)) * eye_rows
    for iteration in range(ITERS):
        factor = (5.0 * eye_full - moment_full) * 0.25
        square = product(factor, factor)
        fourth_rows = product(square, square)
        moment_rows = product(fourth_rows, moment_full)
        iterate = product(iterate, factor)
        if iteration + 1 < ITERS:
            moment_full = collect(moment_rows)
    return iterate.astype(jnp.bfloat16)


def body(gradient, left_stats, right_stats, left_roots, right_roots, refresh):
    position = lax.axis_index("bcol")
    half = position % 2
    block_col = position // 2
    order_size = left_stats.shape[2]
    half_rows = order_size // 2
    is_second = half == 1
    mine = lax.all_to_all(gradient, "bcol", split_axis=1, concat_axis=0, tiled=True)
    left_root_mine = left_roots[0]
    partner_grad, partner_left = from_partner((mine, left_root_mine), "bcol", 0)
    grad_full = jnp.where(
        is_second,
        jnp.concatenate([partner_grad, mine], 1),
        jnp.concatenate([mine, partner_grad], 1),
    )
    left_root_full = jnp.where(
        is_second,
        jnp.concatenate([partner_left, left_root_mine], 0),
        jnp.concatenate([left_root_mine, partner_left], 0),
    )
    grad_rows = lax.dynamic_slice_in_dim(grad_full, half * half_rows, half_rows, 0)
    left_gram = lax.dot_general(
        grad_rows, grad_full, (((1,), (1,)), ((), ())), preferred_element_type=jnp.float32
    )
    right_gram = lax.dot_general(
        mine, grad_full, (((0,), (0,)), ((), ())), preferred_element_type=jnp.float32
    )
    left_new = decay * left_stats[0] + (1.0 - decay) * left_gram
    right_new = decay * right_stats[0] + (1.0 - decay) * right_gram
    right_part = lax.dot_general(
        grad_full, right_roots[0], (((1,), (1,)), ((), ())), preferred_element_type=jnp.float32
    ).astype(jnp.bfloat16)
    update_cols = jnp.dot(left_root_full, right_part, preferred_element_type=jnp.float32).astype(
        jnp.bfloat16
    )
    update = lax.all_to_all(update_cols, "bcol", split_axis=0, concat_axis=1, tiled=True)
    chosen = refresh[0]
    listed = jnp.any(chosen == block_col)
    mine_side = jnp.where(is_second, right_new, left_new)
    partner_side = from_partner(
        jnp.where(is_second, left_new, right_new).astype(jnp.bfloat16), "bcol", 0
    ).astype(jnp.float32)
    whole_side = jnp.where(
        is_second,
        jnp.concatenate([partner_side, mine_side], 0),
        jnp.concatenate([mine_side, partner_side], 0),
    )
    root_full = inverse_rows(whole_side, unchanged)
    own_rows = lax.dynamic_slice_in_dim(root_full, half * half_rows, half_rows, 0)
    given_rows = lax.dynamic_slice_in_dim(root_full, (1 - half) * half_rows, half_rows, 0)
    taken = from_partner(given_rows, "bcol", 0)
    left_fresh = jnp.where(is_second, taken, own_rows)
    right_fresh = jnp.where(is_second, own_rows, taken)
    left_out = jnp.where(listed, left_fresh, left_roots[0])
    right_out = jnp.where(listed, right_fresh, right_roots[0])
    return (update, left_new[None], right_new[None], left_out[None], right_out[None])


def solution(mesh):
    in_specs = (
        P(("brow", "bcol"), None),
        P("brow", "bcol", None),
        P("brow", "bcol", None),
        P("brow", "bcol", None),
        P("brow", "bcol", None),
        P("brow", None),
    )
    out_specs = (
        P(("brow", "bcol"), None),
        P("brow", "bcol", None),
        P("brow", "bcol", None),
        P("brow", "bcol", None),
        P("brow", "bcol", None),
    )
    return jax.shard_map(body, mesh=mesh, in_specs=in_specs, out_specs=out_specs, check_vma=False)
```

profile of v0, /device:TPU:0, one launch (start us, length us, event | category | flops | bytes accessed | tf_op | source)
XLA Modules:
  0.0 51.4 jit_solution(1072921021482301779)
XLA Ops:
  0.6 1.7 %copy.16 = bf16[8,8,8,256]{3,2,0,1:T(8,128)(2,1)} copy(bf16[8,8,8,256]{3,2,1,0:T(8,128)(2,1)} %bitcast.59) | data formatting | bytes 524288 | tf_op jit(solution)/shard_map/all_to_all | solution.py:54
  2.3 0.0 copy-start.3
  2.3 0.0 copy-start.5
  2.3 6.5 %all-to-all-start = ((bf16[64,8,256]{2,0,1:T(8,128)(2,1)}), bf16[64,8,256]{2,0,1:T(8,128)(2,1)S(1)}, u32[]{:S(2)}, u32[]{:S(2)}) async-start(bf16[64,8,256]{2,0,1:T(8,128)(2,1)} %bitcast.48), calls=%async_computation | async-start | bytes 524288 | tf_op jit(solution)/shard_map/all_to_all | solution.py:54
  8.8 0.0 copy-done.3
  8.8 0.5 collective-permute-start
  9.3 9.2 %all-to-all-done = bf16[64,8,256]{2,0,1:T(8,128)(2,1)S(1)} async-done(((bf16[64,8,256]{2,0,1:T(8,128)(2,1)}), bf16[64,8,256]{2,0,1:T(8,128)(2,1)S(1)}, u32[]{:S(2)}, u32[]{:S(2)}) %all-to-all-start) | async-done | bytes 262176 | tf_op jit(solution)/shard_map/all_to_all | solution.py:54
  18.5 0.0 collective-permute-start.1
  18.5 0.0 collective-permute-done
  18.5 1.5 %collective-permute-done.1 = bf16[512,256]{1,0:T(8,128)(2,1)S(1)} collective-permute-done((bf16[512,256]{1,0:T(8,128)(2,1)S(1)}, bf16[512,256]{1,0:T(8,128)(2,1)S(1)}, u32[]{:S(2)}, u32[]{:S(2)}) %collective-permute-start.1) | collective-permute-done | bytes 262176 | tf_op jit(solution)/shard_map/ppermute | solution.py:13
  20.0 0.0 copy-done.5
  20.0 1.5 %convolution_convert_fusion.1 = bf16[512,256]{1,0:T(8,128)(2,1)} fusion(bf16[256,512]{1,0:T(8,128)(2,1)S(1)} %bitcast.58, bf16[256,512]{1,0:T(8,128)(2,1)S(1)} %collective-permute-done, pred[]{:T(512)S(6)} %eq.23, bf16[1,256,512]{2,1,0:T(8,128)(2,1)S(1)} %copy-done.5, bf16[512,256]{1,0:T(8,128)(2,1)S(1)} %bitcast.54, ...), kind=kOutput, calls=%fused_computation.10 | convolution fusion | flops 273416192 | bytes 1572865 | tf_op jit(solution)/shard_map/dot_general | solution.py:79
  21.5 3.4 %all-to-all-start.1 = ((bf16[8,64,256]{2,1,0:T(8,128)(2,1)}), bf16[8,64,256]{2,1,0:T(8,128)(2,1)S(1)}, u32[]{:S(2)}, u32[]{:S(2)}) async-start(bf16[8,64,256]{2,1,0:T(8,128)(2,1)} %bitcast.5), calls=%async_computation.1 | async-start | bytes 524288 | tf_op jit(solution)/shard_map/all_to_all | solution.py:82
  24.9 0.0 copy-start.7
  25.0 0.1 maximum_select_fusion.3
  25.1 0.9 %copy-done.7 = f32[1,256,512]{2,1,0:T(8,128)S(1)} copy-done((f32[1,256,512]{2,1,0:T(8,128)S(1)}, f32[1,256,512]{2,1,0:T(8,128)}, u32[]{:S(2)}) %copy-start.7) | copy-done | bytes 524312
  26.0 0.0 copy-start.2
  26.0 0.3 fusion.2
  26.3 0.7 %copy-done.2 = f32[1,256,512]{2,1,0:T(8,128)S(1)} copy-done((f32[1,256,512]{2,1,0:T(8,128)S(1)}, f32[1,256,512]{2,1,0:T(8,128)}, u32[]{:S(2)}) %copy-start.2) | copy-done | bytes 524312
  27.0 0.0 copy-start
  27.0 0.4 select_convert_fusion
  27.4 0.0 copy-start.1
  27.4 0.5 collective-permute-start.2
  27.9 0.0 copy-done
  27.9 0.1 broadcast_select_fusion
  28.0 0.2 copy-done.1
  28.2 0.8 %collective-permute-done.2 = bf16[256,512]{1,0:T(8,128)(2,1)S(1)} collective-permute-done((bf16[256,512]{1,0:T(8,128)(2,1)S(1)}, bf16[256,512]{1,0:T(8,128)(2,1)S(1)}, u32[]{:S(2)}, u32[]{:S(2)}) %collective-permute-start.2) | collective-permute-done | bytes 262176 | tf_op jit(solution)/shard_map/ppermute | solution.py:13
  29.1 0.9 %multiply_reduce_fusion = f32[]{:T(128)} fusion(f32[256,512]{1,0:T(8,128)S(1)} %convert_element_type.20, f32[256,512]{1,0:T(8,128)S(1)} %broadcast_select_fusion, pred[]{:T(512)S(6)} %eq.23), kind=kLoop, calls=%fused_computation.18 | loop fusion | flops 2097151 | bytes 1048581 | tf_op jit(solution)/shard_map/reduce_sum | solution.py:33
  30.7 2.1 %fusion.15 = f32[512,512]{1,0:T(8,128)S(1)} fusion(f32[]{:T(128)S(6)} %div.14, f32[256,512]{1,0:T(8,128)S(1)} %broadcast_select_fusion, f32[256,512]{1,0:T(8,128)S(1)} %convert_element_type.20, pred[]{:T(512)S(6)} %eq.23), kind=kOutput, calls=%fused_computation.24 | convolution fusion | flops 1613234176 | bytes 2097157 | tf_op jit(solution)/shard_map/dot_general | solution.py:17
  32.8 1.9 %fusion.7 = f32[512,512]{1,0:T(8,128)S(1)} fusion(f32[]{:T(128)S(6)} %div.14, f32[]{:T(128)S(6)} %sqrt.11, f32[256,512]{1,0:T(8,128)S(1)} %broadcast_select_fusion, f32[256,512]{1,0:T(8,128)S(1)} %convert_element_type.20, pred[]{:T(512)S(6)} %eq.23), kind=kOutput, calls=%fused_computation.16 | convolution fusion | flops 1613758464 | bytes 2097161 | tf_op jit(solution)/shard_map/dot_general | solution.py:17
  34.8 1.8 %fusion.61 = f32[512,512]{1,0:T(8,128)S(1)} fusion(f32[512,512]{1,0:T(8,128)S(1)} %fusion.15), kind=kOutput, calls=%fused_computation.72 | convolution fusion | flops 1610612736 | bytes 2097152 | tf_op jit(solution)/shard_map/dot_general | solution.py:17
  36.6 1.9 %fusion.9 = f32[512,512]{1,0:T(8,128)S(1)} fusion(f32[512,512]{1,0:T(8,128)S(1)} %fusion.61, f32[]{:T(128)S(6)} %div.14, f32[256,512]{1,0:T(8,128)S(1)} %broadcast_select_fusion, f32[256,512]{1,0:T(8,128)S(1)} %convert_element_type.20, pred[]{:T(512)S(6)} %eq.23), kind=kOutput, calls=%fused_computation.20 | convolution fusion | flops 1612447744 | bytes 3145733 | tf_op jit(solution)/shard_map/dot_general | solution.py:17
  38.6 1.9 %fusion.11 = f32[512,512]{1,0:T(8,128)S(1)} fusion(f32[512,512]{1,0:T(8,128)S(1)} %fusion.9), kind=kOutput, calls=%fused_computation.22 | convolution fusion | flops 1611661312 | bytes 2097152 | tf_op jit(solution)/shard_map/dot_general | solution.py:17
  40.5 1.9 %fusion.13 = f32[512,512]{1,0:T(8,128)S(1)} fusion(f32[512,512]{1,0:T(8,128)S(1)} %fusion.7, f32[512,512]{1,0:T(8,128)S(1)} %fusion.9), kind=kOutput, calls=%fused_computation.23 | convolution fusion | flops 1611661312 | bytes 3145728 | tf_op jit(solution)/shard_map/dot_general | solution.py:17
  42.4 2.0 %fusion.62 = f32[512,512]{1,0:T(8,128)S(1)} fusion(f32[512,512]{1,0:T(8,128)S(1)} %fusion.11), kind=kOutput, calls=%fused_computation.73 | convolution fusion | flops 1610612736 | bytes 2097152 | tf_op jit(solution)/shard_map/dot_general | solution.py:17
  44.5 1.9 %fusion = f32[512,512]{1,0:T(8,128)S(1)} fusion(f32[512,512]{1,0:T(8,128)S(1)} %fusion.62, f32[512,512]{1,0:T(8,128)S(1)} %fusion.9), kind=kOutput, calls=%fused_computation.3 | convolution fusion | flops 1611661312 | bytes 3145728 | tf_op jit(solution)/shard_map/dot_general | solution.py:17
  46.3 1.9 %convolution_convert_fusion = bf16[512,512]{1,0:T(8,128)(2,1)S(1)} fusion(f32[512,512]{1,0:T(8,128)S(1)} %fusion.13, f32[512,512]{1,0:T(8,128)S(1)} %fusion), kind=kOutput, calls=%fused_computation.4 | convolution fusion | flops 1610874880 | bytes 2621440 | tf_op jit(solution)/shard_map/dot_general | solution.py:17
  48.2 0.4 collective-permute-start.3
  49.3 0.0 all-to-all-done.1
  49.4 0.0 copy-start.4
  49.4 0.0 copy-start.6
  49.4 0.7 %copy.14 = bf16[8,8,8,256]{3,2,0,1:T(8,128)(2,1)} copy(bf16[8,8,8,256]{3,2,1,0:T(8,128)(2,1)S(1)} %bitcast.52) | data formatting | bytes 524288 | tf_op jit(solution)/shard_map/all_to_all | solution.py:82
  50.1 0.0 collective-permute-done.3
  50.1 0.3 copy-done.4
  50.4 0.1 copy-done.6
  50.5 0.9 %fusion.42 = (bf16[1,256,512]{2,1,0:T(8,128)(2,1)}, bf16[1,256,512]{2,1,0:T(8,128)(2,1)}) fusion(bf16[1,256,512]{2,1,0:T(8,128)(2,1)S(1)} %copy-done.6, bf16[256,512]{1,0:T(8,128)(2,1)S(1)} %collective-permute-done.3, pred[]{:T(512)S(6)} %eq.23, pred[]{:T(512)} %bitcast.14, bf16[512,512]{1,0:T(8,128)(2,1)S(1)} %convolution_convert_fusion, s32[]{:T(128)S(6)} %select_n.72, ...), kind=kLoop, calls=%fused_computation.53 | loop fusion | flops 524288 | bytes 1572870 | tf_op jit(solution)/shard_map/broadcast_in_dim | solution.py:102
  (2 shorter events, 0.1 us)
Async XLA Ops:
  2.3 6.5 %copy-start.3 = (bf16[1,256,512]{2,1,0:T(8,128)(2,1)S(1)}, bf16[1,256,512]{2,1,0:T(8,128)(2,1)}, u32[]{:S(2)}) copy-start(bf16[1,256,512]{2,1,0:T(8,128)(2,1)} %param.9) | copy-start | bytes 786436
  2.3 17.7 %copy-start.5 = (bf16[1,256,512]{2,1,0:T(8,128)(2,1)S(1)}, bf16[1,256,512]{2,1,0:T(8,128)(2,1)}, u32[]{:S(2)}) copy-start(bf16[1,256,512]{2,1,0:T(8,128)(2,1)} %param.10) | copy-start | bytes 786436
  2.3 16.2 %all-to-all-start = ((bf16[64,8,256]{2,0,1:T(8,128)(2,1)}), bf16[64,8,256]{2,0,1:T(8,128)(2,1)S(1)}, u32[]{:S(2)}, u32[]{:S(2)}) async-start(bf16[64,8,256]{2,0,1:T(8,128)(2,1)} %bitcast.48), calls=%async_computation | async-start | bytes 524288 | tf_op jit(solution)/shard_map/all_to_all | solution.py:54
  8.8 9.7 %collective-permute-start = (bf16[256,512]{1,0:T(8,128)(2,1)S(1)}, bf16[256,512]{1,0:T(8,128)(2,1)S(1)}, u32[]{:S(2)}, u32[]{:S(2)}) collective-permute-start(bf16[256,512]{1,0:T(8,128)(2,1)S(1)} %bitcast.57), channel_id=1, source_target_pairs={{0,1},{1,0},{2,3},{3,2},{4,5},{5,4},{6,7},{7,6},{8,9},{9,8},{10,11... | collective-permute-start | bytes 786440 | tf_op jit(solution)/shard_map/ppermute | solution.py:13
  18.5 1.5 %collective-permute-start.1 = (bf16[512,256]{1,0:T(8,128)(2,1)S(1)}, bf16[512,256]{1,0:T(8,128)(2,1)S(1)}, u32[]{:S(2)}, u32[]{:S(2)}) collective-permute-start(bf16[512,256]{1,0:T(8,128)(2,1)S(1)} %bitcast.53), channel_id=1, source_target_pairs={{0,1},{1,0},{2,3},{3,2},{4,5},{5,4},{6,7},{7,6},{8,9},{9,8},{10,11... | collective-permute-start | bytes 786440 | tf_op jit(solution)/shard_map/ppermute | solution.py:13
  21.5 27.8 %all-to-all-start.1 = ((bf16[8,64,256]{2,1,0:T(8,128)(2,1)}), bf16[8,64,256]{2,1,0:T(8,128)(2,1)S(1)}, u32[]{:S(2)}, u32[]{:S(2)}) async-start(bf16[8,64,256]{2,1,0:T(8,128)(2,1)} %bitcast.5), calls=%async_computation.1 | async-start | bytes 524288 | tf_op jit(solution)/shard_map/all_to_all | solution.py:82
  24.9 1.0 %copy-start.7 = (f32[1,256,512]{2,1,0:T(8,128)S(1)}, f32[1,256,512]{2,1,0:T(8,128)}, u32[]{:S(2)}) copy-start(f32[1,256,512]{2,1,0:T(8,128)} %param.8) | copy-start | bytes 1572868
  26.0 1.0 %copy-start.2 = (f32[1,256,512]{2,1,0:T(8,128)S(1)}, f32[1,256,512]{2,1,0:T(8,128)}, u32[]{:S(2)}) copy-start(f32[1,256,512]{2,1,0:T(8,128)} %param.7) | copy-start | bytes 1572868
  27.0 0.8 %copy-start = (f32[256,512]{1,0:T(8,128)}, f32[256,512]{1,0:T(8,128)S(1)}, u32[]{:S(2)}) copy-start(f32[256,512]{1,0:T(8,128)S(1)} %fusion.2) | copy-start | bytes 1572868
  27.4 0.8 %copy-start.1 = (f32[256,512]{1,0:T(8,128)}, f32[256,512]{1,0:T(8,128)S(1)}, u32[]{:S(2)}) copy-start(f32[256,512]{1,0:T(8,128)S(1)} %get-tuple-element.8) | copy-start | bytes 1572868
  27.4 1.6 %collective-permute-start.2 = (bf16[256,512]{1,0:T(8,128)(2,1)S(1)}, bf16[256,512]{1,0:T(8,128)(2,1)S(1)}, u32[]{:S(2)}, u32[]{:S(2)}) collective-permute-start(bf16[256,512]{1,0:T(8,128)(2,1)S(1)} %get-tuple-element.7), channel_id=1, source_target_pairs={{0,1},{1,0},{2,3},{3,2},{4,5},{5,4},{6,7},{7,6},{8,9},{9,8},{10,11... | collective-permute-start | bytes 786440 | tf_op jit(solution)/shard_map/ppermute | solution.py:13
  48.2 1.9 %collective-permute-start.3 = (bf16[256,512]{1,0:T(8,128)(2,1)S(1)}, bf16[256,512]{1,0:T(8,128)(2,1)S(1)}, u32[]{:S(2)}, u32[]{:S(2)}) collective-permute-start(bf16[256,512]{1,0:T(8,128)(2,1)S(1)} %constant_dynamic-slice_fusion), channel_id=1, source_target_pairs={{0,1},{1,0},{2,3},{3,2},{4,5},{5,4},{6,7},{7,6},{8,9},{9,8},{10,11... | collective-permute-start | bytes 786440 | tf_op jit(solution)/shard_map/ppermute | solution.py:13
  49.4 1.0 %copy-start.4 = (bf16[1,256,512]{2,1,0:T(8,128)(2,1)S(1)}, bf16[1,256,512]{2,1,0:T(8,128)(2,1)}, u32[]{:S(2)}) copy-start(bf16[1,256,512]{2,1,0:T(8,128)(2,1)} %param.9) | copy-start | bytes 786436
  49.4 1.1 %copy-start.6 = (bf16[1,256,512]{2,1,0:T(8,128)(2,1)S(1)}, bf16[1,256,512]{2,1,0:T(8,128)(2,1)}, u32[]{:S(2)}) copy-start(bf16[1,256,512]{2,1,0:T(8,128)(2,1)} %param.10) | copy-start | bytes 786436
where the time goes:
time: 51.9 us; the launch traced here: 51.4 us
  matrix products  19.5 us (38%)
  waiting for transfers between devices  11.6 us (22%)
  starting transfers between devices  11.3 us (22%)
  local copies, waits for them, and re-layouts  4.65 us (9%)
  between operations  2.24 us (4%)
  other arithmetic  2.1 us (4%)
    dot_general x9, matrix products, product(): return jnp.dot(left_side, right_side, precision=highest)  17.4 us
    all_to_all x1, waiting for transfers between devices, body(): lax.all_to_all(gradient, 'bcol', split_axis=1, concat_axis=0, tiled=True)  9.2 us
    all_to_all x1, starting transfers between devices, body(): lax.all_to_all(gradient, 'bcol', split_axis=1, concat_axis=0, tiled=True)  6.49 us
    all_to_all x1, starting transfers between devices, body(): lax.all_to_all(update_cols, 'bcol', split_axis=0, concat_axis=1, tiled=True)  3.41 us
    ppermute x4, waiting for transfers between devices, from_partner(): lax.ppermute(shard, axis, [(i, i ^ 1 << stride) for i in range(lax.axis_s...  2.38 us
    unnamed x16, local copies, waits for them, and re-layouts  2.23 us
    all_to_all x1, local copies, waits for them, and re-layouts, body(): lax.all_to_all(gradient, 'bcol', split_axis=1, concat_axis=0, tiled=True)  1.67 us
    dot_general x1, matrix products, body(): jnp.dot(left_root_full, right_part, preferred_element_type=jnp.float32)  1.48 us
  transfers between devices with their start and end apart: 6, of which 3 were waited for; matrix products, arithmetic and copies ran while one was open for 39% of the time, Pallas kernels for 0%

commit v1 on v0

--- a/solution.py
+++ b/solution.py
@@ -45,6 +45,19 @@
 
 
 def body(gradient, left_stats, right_stats, left_roots, right_roots, refresh):
+
+    def hold_sites(vals, across):
+        y1 = jnp.concatenate(
+            lax.all_to_all(
+                jnp.stack(jnp.split(vals, lax.axis_size(across), axis=0)),
+                axis_name=across,
+                split_axis=0,
+                concat_axis=0,
+            ),
+            axis=1,
+        )
+        return y1
+
     position = lax.axis_index("bcol")
     half = position % 2
     block_col = position // 2
@@ -79,7 +92,7 @@
     update_cols = jnp.dot(left_root_full, right_part, preferred_element_type=jnp.float32).astype(
         jnp.bfloat16
     )
-    update = lax.all_to_all(update_cols, "bcol", split_axis=0, concat_axis=1, tiled=True)
+    update = hold_sites(update_cols, "bcol")
     chosen = refresh[0]
     listed = jnp.any(chosen == block_col)
     mine_side = jnp.where(is_second, right_new, left_new)

time: 51.9 us -> 56.2 us (1.083)
  local copies, waits for them, and re-layouts: 4.65 us -> 9.58 us
  matrix products: 19.5 us -> 18.8 us
    unnamed x16 -> x23, local copies, waits for them, and re-layouts: 2.23 us -> 6.55 us
    all_to_all x1 -> x0, local copies, waits for them, and re-layouts: 0.72 us -> none  [body(): lax.all_to_all(update_cols, 'bcol', split_axis=0, concat_axis=1, tiled=True)]
    reshape x0 -> x1, local copies, waits for them, and re-layouts: none -> 0.72 us  [hold_sites(): jnp.concatenate(lax.all_to_all(jnp.stack(jnp.split(vals, lax.axis_size(ac...]
    dot_general x1, matrix products: 1.48 us -> 0.77 us  [body(): jnp.dot(left_root_full, right_part, preferred_element_type=jnp.float32)]
    another operation x0 -> x1, local copies, waits for them, and re-layouts: none -> 0.62 us  [hold_sites(): jnp.stack(jnp.split(vals, lax.axis_size(across), axis=0))]
  transfers between devices with their start and end apart: 6 -> 6, of which waited for: 3 -> 3; matrix products, arithmetic and copies ran while one was open for 39% -> 36% of each run, Pallas kernels for 0% -> 0%
where the time goes in v1:
time: 56.2 us; the launch traced here: 55.7 us
  matrix products  18.8 us (33%)
  waiting for transfers between devices  11.6 us (21%)
  starting transfers between devices  11.3 us (20%)
  local copies, waits for them, and re-layouts  9.58 us (17%)
  between operations  2.25 us (4%)
  other arithmetic  2.1 us (4%)
    dot_general x9, matrix products, product(): return jnp.dot(left_side, right_side, precision=highest)  17.4 us
    all_to_all x1, waiting for transfers between devices, body(): lax.all_to_all(gradient, 'bcol', split_axis=1, concat_axis=0, tiled=True)  9.2 us
    unnamed x23, local copies, waits for them, and re-layouts  6.55 us
    all_to_all x1, starting transfers between devices, body(): lax.all_to_all(gradient, 'bcol', split_axis=1, concat_axis=0, tiled=True)  6.49 us
    all_to_all x1, starting transfers between devices, hold_sites(): lax.all_to_all(jnp.stack(jnp.split(vals, lax.axis_size(across), axis=0)),...  3.41 us
    ppermute x4, waiting for transfers between devices, from_partner(): lax.ppermute(shard, axis, [(i, i ^ 1 << stride) for i in range(lax.axis_s...  2.38 us
    all_to_all x1, local copies, waits for them, and re-layouts, body(): lax.all_to_all(gradient, 'bcol', split_axis=1, concat_axis=0, tiled=True)  1.67 us
    ppermute x4, starting transfers between devices, from_partner(): lax.ppermute(shard, axis, [(i, i ^ 1 << stride) for i in range(lax.axis_s...  1.4 us
  transfers between devices with their start and end apart: 6, of which 3 were waited for; matrix products, arithmetic and copies ran while one was open for 36% of the time, Pallas kernels for 0%

profile of v1, /device:TPU:0, one launch (start us, length us, event | category | flops | bytes accessed | tf_op | source)
XLA Modules:
  0.0 55.7 jit_solution(8330460665176747677)
XLA Ops:
  0.6 1.7 %copy.17 = bf16[8,8,8,256]{3,2,0,1:T(8,128)(2,1)} copy(bf16[8,8,8,256]{3,2,1,0:T(8,128)(2,1)} %bitcast.90) | data formatting | bytes 524288 | tf_op jit(solution)/shard_map/all_to_all | solution.py:67
  2.3 6.5 %all-to-all-start = ((bf16[64,8,256]{2,0,1:T(8,128)(2,1)}), bf16[64,8,256]{2,0,1:T(8,128)(2,1)S(1)}, u32[]{:S(2)}, u32[]{:S(2)}) async-start(bf16[64,8,256]{2,0,1:T(8,128)(2,1)} %bitcast.79), calls=%async_computation | async-start | bytes 524288 | tf_op jit(solution)/shard_map/all_to_all | solution.py:67
  8.8 0.0 copy-done.3
  8.8 0.5 collective-permute-start
  9.3 9.2 %all-to-all-done = bf16[64,8,256]{2,0,1:T(8,128)(2,1)S(1)} async-done(((bf16[64,8,256]{2,0,1:T(8,128)(2,1)}), bf16[64,8,256]{2,0,1:T(8,128)(2,1)S(1)}, u32[]{:S(2)}, u32[]{:S(2)}) %all-to-all-start) | async-done | bytes 262176 | tf_op jit(solution)/shard_map/all_to_all | solution.py:67
  18.5 0.0 collective-permute-start.1
  18.5 0.0 collective-permute-done
  18.5 1.5 %collective-permute-done.1 = bf16[512,256]{1,0:T(8,128)(2,1)S(1)} collective-permute-done((bf16[512,256]{1,0:T(8,128)(2,1)S(1)}, bf16[512,256]{1,0:T(8,128)(2,1)S(1)}, u32[]{:S(2)}, u32[]{:S(2)}) %collective-permute-start.1) | collective-permute-done | bytes 262176 | tf_op jit(solution)/shard_map/ppermute | solution.py:13
  20.0 0.8 %convolution_convert_fusion.1 = bf16[512,256]{1,0:T(8,128)(2,1)S(1)} fusion(bf16[256,512]{1,0:T(8,128)(2,1)S(1)} %bitcast.89, bf16[256,512]{1,0:T(8,128)(2,1)S(1)} %collective-permute-done, pred[]{:T(512)S(6)} %eq.23, bf16[1,256,512]{2,1,0:T(8,128)(2,1)S(1)} %copy-done.5, bf16[512,256]{1,0:T(8,128)(2,1)S(1)} %bitcast.85, ...), kind=kOutput, calls=%fused_computation.10 | convolution fusion | flops 273416192 | bytes 1572865 | tf_op jit(solution)/shard_map/dot_general | solution.py:92
  20.8 0.6 %fusion.51 = bf16[8,64,256]{2,1,0:T(8,128)(2,1)} fusion(bf16[512,256]{1,0:T(8,128)(2,1)S(1)} %convolution_convert_fusion.1), kind=kLoop, calls=%fused_computation.72 | loop fusion | bytes 65536
  21.4 0.6 %fusion.50 = bf16[8,64,256]{2,1,0:T(8,128)(2,1)} fusion(bf16[8,64,256]{2,1,0:T(8,128)(2,1)} %fusion.51, bf16[512,256]{1,0:T(8,128)(2,1)S(1)} %convolution_convert_fusion.1), kind=kLoop, calls=%fused_computation.70 | loop fusion | bytes 65536
  22.1 0.6 %fusion.49 = bf16[8,64,256]{2,1,0:T(8,128)(2,1)} fusion(bf16[8,64,256]{2,1,0:T(8,128)(2,1)} %fusion.50, bf16[512,256]{1,0:T(8,128)(2,1)S(1)} %convolution_convert_fusion.1), kind=kLoop, calls=%fused_computation.68 | loop fusion | bytes 65536
  22.7 0.6 %fusion.48 = bf16[8,64,256]{2,1,0:T(8,128)(2,1)} fusion(bf16[8,64,256]{2,1,0:T(8,128)(2,1)} %fusion.49, bf16[512,256]{1,0:T(8,128)(2,1)S(1)} %convolution_convert_fusion.1), kind=kLoop, calls=%fused_computation.66 | loop fusion | bytes 65536
  23.3 0.6 %fusion.47 = bf16[8,64,256]{2,1,0:T(8,128)(2,1)} fusion(bf16[8,64,256]{2,1,0:T(8,128)(2,1)} %fusion.48, bf16[512,256]{1,0:T(8,128)(2,1)S(1)} %convolution_convert_fusion.1), kind=kLoop, calls=%fused_computation.64 | loop fusion | bytes 65536
  23.9 0.6 %fusion.46 = bf16[8,64,256]{2,1,0:T(8,128)(2,1)} fusion(bf16[8,64,256]{2,1,0:T(8,128)(2,1)} %fusion.47, bf16[512,256]{1,0:T(8,128)(2,1)S(1)} %convolution_convert_fusion.1), kind=kLoop, calls=%fused_computation.62 | loop fusion | bytes 65536
  24.5 0.6 %fusion.45 = bf16[8,64,256]{2,1,0:T(8,128)(2,1)} fusion(bf16[8,64,256]{2,1,0:T(8,128)(2,1)} %fusion.46, bf16[512,256]{1,0:T(8,128)(2,1)S(1)} %convolution_convert_fusion.1), kind=kLoop, calls=%fused_computation.60 | loop fusion | bytes 65536
  25.1 0.6 %fusion.44 = bf16[8,64,256]{2,1,0:T(8,128)(2,1)} fusion(bf16[8,64,256]{2,1,0:T(8,128)(2,1)} %fusion.45, bf16[512,256]{1,0:T(8,128)(2,1)S(1)} %convolution_convert_fusion.1), kind=kLoop, calls=%fused_computation.58 | loop fusion | bytes 65536 | tf_op jit(solution)/shard_map/stack | solution.py:52
  25.8 3.4 %all-to-all-start.1 = ((bf16[8,64,256]{2,1,0:T(8,128)(2,1)}), bf16[8,64,256]{2,1,0:T(8,128)(2,1)S(1)}, u32[]{:S(2)}, u32[]{:S(2)}) async-start(bf16[8,64,256]{2,1,0:T(8,128)(2,1)} %fusion.44), calls=%async_computation.1 | async-start | bytes 524288 | tf_op jit(solution)/shard_map/all_to_all | solution.py:51
  29.2 0.0 copy-start.7
  29.2 0.1 maximum_select_fusion.3
  29.3 0.9 %copy-done.7 = f32[1,256,512]{2,1,0:T(8,128)S(1)} copy-done((f32[1,256,512]{2,1,0:T(8,128)S(1)}, f32[1,256,512]{2,1,0:T(8,128)}, u32[]{:S(2)}) %copy-start.7) | copy-done | bytes 524312
  30.2 0.3 fusion.2
  30.6 0.7 %copy-done.2 = f32[1,256,512]{2,1,0:T(8,128)S(1)} copy-done((f32[1,256,512]{2,1,0:T(8,128)S(1)}, f32[1,256,512]{2,1,0:T(8,128)}, u32[]{:S(2)}) %copy-start.2) | copy-done | bytes 524312
  31.3 0.4 select_convert_fusion
  31.6 0.0 copy-start.1
  31.6 0.5 collective-permute-start.2
  32.1 0.1 broadcast_select_fusion
  32.2 0.2 copy-done.1
  32.4 0.8 %collective-permute-done.2 = bf16[256,512]{1,0:T(8,128)(2,1)S(1)} collective-permute-done((bf16[256,512]{1,0:T(8,128)(2,1)S(1)}, bf16[256,512]{1,0:T(8,128)(2,1)S(1)}, u32[]{:S(2)}, u32[]{:S(2)}) %collective-permute-start.2) | collective-permute-done | bytes 262176 | tf_op jit(solution)/shard_map/ppermute | solution.py:13
  33.3 0.9 %multiply_reduce_fusion = f32[]{:T(128)} fusion(f32[256,512]{1,0:T(8,128)S(1)} %convert_element_type.20, f32[256,512]{1,0:T(8,128)S(1)} %broadcast_select_fusion, pred[]{:T(512)S(6)} %eq.23), kind=kLoop, calls=%fused_computation.18 | loop fusion | flops 2097151 | bytes 1048581 | tf_op jit(solution)/shard_map/reduce_sum | solution.py:33
  35.0 2.1 %fusion.15 = f32[512,512]{1,0:T(8,128)S(1)} fusion(f32[]{:T(128)S(6)} %div.14, f32[256,512]{1,0:T(8,128)S(1)} %broadcast_select_fusion, f32[256,512]{1,0:T(8,128)S(1)} %convert_element_type.20, pred[]{:T(512)S(6)} %eq.23), kind=kOutput, calls=%fused_computation.24 | convolution fusion | flops 1613234176 | bytes 2097157 | tf_op jit(solution)/shard_map/dot_general | solution.py:17
  37.1 1.9 %fusion.7 = f32[512,512]{1,0:T(8,128)S(1)} fusion(f32[]{:T(128)S(6)} %div.14, f32[]{:T(128)S(6)} %sqrt.11, f32[256,512]{1,0:T(8,128)S(1)} %broadcast_select_fusion, f32[256,512]{1,0:T(8,128)S(1)} %convert_element_type.20, pred[]{:T(512)S(6)} %eq.23), kind=kOutput, calls=%fused_computation.16 | convolution fusion | flops 1613758464 | bytes 2097161 | tf_op jit(solution)/shard_map/dot_general | solution.py:17
  39.0 1.8 %fusion.69 = f32[512,512]{1,0:T(8,128)S(1)} fusion(f32[512,512]{1,0:T(8,128)S(1)} %fusion.15), kind=kOutput, calls=%fused_computation.88 | convolution fusion | flops 1610612736 | bytes 2097152 | tf_op jit(solution)/shard_map/dot_general | solution.py:17
  40.9 1.9 %fusion.9 = f32[512,512]{1,0:T(8,128)S(1)} fusion(f32[512,512]{1,0:T(8,128)S(1)} %fusion.69, f32[]{:T(128)S(6)} %div.14, f32[256,512]{1,0:T(8,128)S(1)} %broadcast_select_fusion, f32[256,512]{1,0:T(8,128)S(1)} %convert_element_type.20, pred[]{:T(512)S(6)} %eq.23), kind=kOutput, calls=%fused_computation.20 | convolution fusion | flops 1612447744 | bytes 3145733 | tf_op jit(solution)/shard_map/dot_general | solution.py:17
  42.8 1.9 %fusion.11 = f32[512,512]{1,0:T(8,128)S(1)} fusion(f32[512,512]{1,0:T(8,128)S(1)} %fusion.9), kind=kOutput, calls=%fused_computation.22 | convolution fusion | flops 1611661312 | bytes 2097152 | tf_op jit(solution)/shard_map/dot_general | solution.py:17
  44.8 1.9 %fusion.13 = f32[512,512]{1,0:T(8,128)S(1)} fusion(f32[512,512]{1,0:T(8,128)S(1)} %fusion.7, f32[512,512]{1,0:T(8,128)S(1)} %fusion.9), kind=kOutput, calls=%fused_computation.23 | convolution fusion | flops 1611661312 | bytes 3145728 | tf_op jit(solution)/shard_map/dot_general | solution.py:17
  46.7 2.0 %fusion.70 = f32[512,512]{1,0:T(8,128)S(1)} fusion(f32[512,512]{1,0:T(8,128)S(1)} %fusion.11), kind=kOutput, calls=%fused_computation.89 | convolution fusion | flops 1610612736 | bytes 2097152 | tf_op jit(solution)/shard_map/dot_general | solution.py:17
  48.7 1.9 %fusion = f32[512,512]{1,0:T(8,128)S(1)} fusion(f32[512,512]{1,0:T(8,128)S(1)} %fusion.70, f32[512,512]{1,0:T(8,128)S(1)} %fusion.9), kind=kOutput, calls=%fused_computation.3 | convolution fusion | flops 1611661312 | bytes 3145728 | tf_op jit(solution)/shard_map/dot_general | solution.py:17
  50.6 1.9 %convolution_convert_fusion = bf16[512,512]{1,0:T(8,128)(2,1)S(1)} fusion(f32[512,512]{1,0:T(8,128)S(1)} %fusion.13, f32[512,512]{1,0:T(8,128)S(1)} %fusion), kind=kOutput, calls=%fused_computation.4 | convolution fusion | flops 1610874880 | bytes 2621440 | tf_op jit(solution)/shard_map/dot_general | solution.py:17
  52.5 0.4 collective-permute-start.3
  53.6 0.0 all-to-all-done.1
  53.6 0.0 copy-start.4
  53.6 0.0 copy-start.6
  53.6 0.7 %copy.15 = bf16[8,8,8,256]{3,2,0,1:T(8,128)(2,1)} copy(bf16[8,8,8,256]{3,2,1,0:T(8,128)(2,1)S(1)} %bitcast.83) | data formatting | bytes 524288 | tf_op jit(solution)/shard_map/reshape | solution.py:50
  54.3 0.0 collective-permute-done.3
  54.3 0.3 copy-done.4
  54.6 0.1 copy-done.6
  54.7 0.9 %fusion.42 = (bf16[1,256,512]{2,1,0:T(8,128)(2,1)}, bf16[1,256,512]{2,1,0:T(8,128)(2,1)}) fusion(bf16[1,256,512]{2,1,0:T(8,128)(2,1)S(1)} %copy-done.6, bf16[256,512]{1,0:T(8,128)(2,1)S(1)} %collective-permute-done.3, pred[]{:T(512)S(6)} %eq.23, pred[]{:T(512)} %bitcast.21, bf16[512,512]{1,0:T(8,128)(2,1)S(1)} %convolution_convert_fusion, s32[]{:T(128)S(6)} %select_n.72, ...), kind=kLoop, calls=%fused_computation.53 | loop fusion | flops 524288 | bytes 1572870 | tf_op jit(solution)/shard_map/broadcast_in_dim | solution.py:115
  (8 shorter events, 0.1 us)
Async XLA Ops:
  2.3 6.5 %copy-start.3 = (bf16[1,256,512]{2,1,0:T(8,128)(2,1)S(1)}, bf16[1,256,512]{2,1,0:T(8,128)(2,1)}, u32[]{:S(2)}) copy-start(bf16[1,256,512]{2,1,0:T(8,128)(2,1)} %param.9) | copy-start | bytes 786436
  2.3 17.7 %copy-start.5 = (bf16[1,256,512]{2,1,0:T(8,128)(2,1)S(1)}, bf16[1,256,512]{2,1,0:T(8,128)(2,1)}, u32[]{:S(2)}) copy-start(bf16[1,256,512]{2,1,0:T(8,128)(2,1)} %param.10) | copy-start | bytes 786436
  2.3 16.2 %all-to-all-start = ((bf16[64,8,256]{2,0,1:T(8,128)(2,1)}), bf16[64,8,256]{2,0,1:T(8,128)(2,1)S(1)}, u32[]{:S(2)}, u32[]{:S(2)}) async-start(bf16[64,8,256]{2,0,1:T(8,128)(2,1)} %bitcast.79), calls=%async_computation | async-start | bytes 524288 | tf_op jit(solution)/shard_map/all_to_all | solution.py:67
  8.8 9.7 %collective-permute-start = (bf16[256,512]{1,0:T(8,128)(2,1)S(1)}, bf16[256,512]{1,0:T(8,128)(2,1)S(1)}, u32[]{:S(2)}, u32[]{:S(2)}) collective-permute-start(bf16[256,512]{1,0:T(8,128)(2,1)S(1)} %bitcast.88), channel_id=1, source_target_pairs={{0,1},{1,0},{2,3},{3,2},{4,5},{5,4},{6,7},{7,6},{8,9},{9,8},{10,11... | collective-permute-start | bytes 786440 | tf_op jit(solution)/shard_map/ppermute | solution.py:13
  18.5 1.5 %collective-permute-start.1 = (bf16[512,256]{1,0:T(8,128)(2,1)S(1)}, bf16[512,256]{1,0:T(8,128)(2,1)S(1)}, u32[]{:S(2)}, u32[]{:S(2)}) collective-permute-start(bf16[512,256]{1,0:T(8,128)(2,1)S(1)} %bitcast.84), channel_id=1, source_target_pairs={{0,1},{1,0},{2,3},{3,2},{4,5},{5,4},{6,7},{7,6},{8,9},{9,8},{10,11... | collective-permute-start | bytes 786440 | tf_op jit(solution)/shard_map/ppermute | solution.py:13
  25.8 27.8 %all-to-all-start.1 = ((bf16[8,64,256]{2,1,0:T(8,128)(2,1)}), bf16[8,64,256]{2,1,0:T(8,128)(2,1)S(1)}, u32[]{:S(2)}, u32[]{:S(2)}) async-start(bf16[8,64,256]{2,1,0:T(8,128)(2,1)} %fusion.44), calls=%async_computation.1 | async-start | bytes 524288 | tf_op jit(solution)/shard_map/all_to_all | solution.py:51
  29.2 1.0 %copy-start.7 = (f32[1,256,512]{2,1,0:T(8,128)S(1)}, f32[1,256,512]{2,1,0:T(8,128)}, u32[]{:S(2)}) copy-start(f32[1,256,512]{2,1,0:T(8,128)} %param.8) | copy-start | bytes 1572868
  30.2 1.0 %copy-start.2 = (f32[1,256,512]{2,1,0:T(8,128)S(1)}, f32[1,256,512]{2,1,0:T(8,128)}, u32[]{:S(2)}) copy-start(f32[1,256,512]{2,1,0:T(8,128)} %param.7) | copy-start | bytes 1572868
  31.3 0.9 %copy-start = (f32[256,512]{1,0:T(8,128)}, f32[256,512]{1,0:T(8,128)S(1)}, u32[]{:S(2)}) copy-start(f32[256,512]{1,0:T(8,128)S(1)} %fusion.2) | copy-start | bytes 1572868
  31.6 0.8 %copy-start.1 = (f32[256,512]{1,0:T(8,128)}, f32[256,512]{1,0:T(8,128)S(1)}, u32[]{:S(2)}) copy-start(f32[256,512]{1,0:T(8,128)S(1)} %get-tuple-element.8) | copy-start | bytes 1572868
  31.6 1.6 %collective-permute-start.2 = (bf16[256,512]{1,0:T(8,128)(2,1)S(1)}, bf16[256,512]{1,0:T(8,128)(2,1)S(1)}, u32[]{:S(2)}, u32[]{:S(2)}) collective-permute-start(bf16[256,512]{1,0:T(8,128)(2,1)S(1)} %get-tuple-element.7), channel_id=1, source_target_pairs={{0,1},{1,0},{2,3},{3,2},{4,5},{5,4},{6,7},{7,6},{8,9},{9,8},{10,11... | collective-permute-start | bytes 786440 | tf_op jit(solution)/shard_map/ppermute | solution.py:13
  52.5 1.8 %collective-permute-start.3 = (bf16[256,512]{1,0:T(8,128)(2,1)S(1)}, bf16[256,512]{1,0:T(8,128)(2,1)S(1)}, u32[]{:S(2)}, u32[]{:S(2)}) collective-permute-start(bf16[256,512]{1,0:T(8,128)(2,1)S(1)} %constant_dynamic-slice_fusion), channel_id=1, source_target_pairs={{0,1},{1,0},{2,3},{3,2},{4,5},{5,4},{6,7},{7,6},{8,9},{9,8},{10,11... | collective-permute-start | bytes 786440 | tf_op jit(solution)/shard_map/ppermute | solution.py:13
  53.6 1.0 %copy-start.4 = (bf16[1,256,512]{2,1,0:T(8,128)(2,1)S(1)}, bf16[1,256,512]{2,1,0:T(8,128)(2,1)}, u32[]{:S(2)}) copy-start(bf16[1,256,512]{2,1,0:T(8,128)(2,1)} %param.9) | copy-start | bytes 786436
  53.6 1.1 %copy-start.6 = (bf16[1,256,512]{2,1,0:T(8,128)(2,1)S(1)}, bf16[1,256,512]{2,1,0:T(8,128)(2,1)}, u32[]{:S(2)}) copy-start(bf16[1,256,512]{2,1,0:T(8,128)(2,1)} %param.10) | copy-start | bytes 786436
